TPU v7x, 32 devices: a whole 2x2x4 slice. The times are simulated.
32 devices in a mesh: gx: 4 (over y, x), gy: 8 (over z, core).
Axes of the slice: x: 2, y: 2, z: 4, core: 2. Of those that a mesh axis runs over, the one named last changes fastest.
Arguments:
- thermal_field: bfloat16 [384, 384, 128], P('gx', 'gy'), may hold values from -6 to 6
- probe_range_east: bfloat16 [384, 128], P('gx'), may hold values from -0.3125 to 0.3125
- probe_range_north: bfloat16 [384, 128], P('gy'), may hold values from -0.3125 to 0.3125
- probe_range_upward: bfloat16 [128, 128], replicated, may hold values from -0.5 to 0.5
- gauss_kernel_east: bfloat16 [384, 384], replicated, may hold values from -0.3125 to 0.3125
- gauss_kernel_north: bfloat16 [384, 384], replicated, may hold values from -0.3125 to 0.3125
- gauss_kernel_upward: bfloat16 [384, 128], replicated, may hold values from -0.5 to 0.5
Outputs:
- factor_x: float32 [384, 128], P('gx')
- factor_y: float32 [384, 128], P('gy')
- factor_z: float32 [128, 128], replicated
- core_sketch: float32 [384, 384, 384], P('gx', None, 'gy')
All inputs are finite; a program needn't handle non-finite values.
Results may differ from a plain program's by a relative error of at most 0.0029.
Values may be sent and summed in bfloat16 or wider, within the bound.
A program may use at most 64 MiB of HBM per device.

v0:
```python
import functools

import jax
import jax.numpy as jnp
import numpy as np
from jax import lax
from jax.experimental import pallas as pl
from jax.experimental.pallas import tpu as pltpu
from jax.sharding import PartitionSpec as P

MESH = pl.DeviceIdType.MESH
VMEM = pl.BlockSpec(memory_space=pltpu.VMEM)
ANY = pl.BlockSpec(memory_space=pl.ANY)
BF = jnp.bfloat16
F32 = jnp.float32


def remote(src, dst, send, recv, where):
    copy = pltpu.make_async_remote_copy(
        src_ref=src, dst_ref=dst, send_sem=send, recv_sem=recv, device_id=where, device_id_type=MESH
    )
    copy.start()
    return copy


def sketch_parts(f_ref, east_ref, north_ref, up_ref, q_ref, py_ref, px_buf):
    rows, span, deep = f_ref.shape
    width = up_ref.shape[1]
    step = 16 if rows % 16 == 0 else rows
    along_y = north_ref[...].astype(F32)
    part_y = jnp.zeros((span, width), F32)
    part_z = jnp.zeros((deep, width), F32)
    for c in range(0, rows, step):
        cells = f_ref[c : c + step].reshape(step * span, deep)
        along_x = east_ref[c : c + step].astype(F32)
        weighted = jnp.dot(cells, up_ref[...], preferred_element_type=F32).reshape(step, span, width)
        px_buf[c : c + step] = jnp.sum(weighted * along_y[None, :, :], axis=1)
        part_y = part_y + jnp.sum(weighted * along_x[:, None, :], axis=0)
        khatri = (along_x[:, None, :] * along_y[None, :, :]).astype(BF).reshape(step * span, width)
        part_z = part_z + lax.dot_general(
            cells, khatri, (((0,), (0,)), ((), ())), preferred_element_type=F32
        )
    py_ref[...] = part_y
    ny = q_ref.shape[0]
    x_rows, z_rows = rows // ny, deep // ny
    for k in range(ny):
        q_ref[k, :x_rows] = px_buf[k * x_rows : (k + 1) * x_rows]
        q_ref[k, x_rows:] = part_z[k * z_rows : (k + 1) * z_rows]


def mix_x_kernel(
    n, chunks, t_ref, g_ref, f_ref, east_ref, north_ref, up_ref, w_ref, q_ref, py_ref,
    x_buf, y_buf, px_buf, s1, r1, s2, r2, ls,
):
    gx, gy = lax.axis_index("gx"), lax.axis_index("gy")
    rows = t_ref.shape[0]
    a_rows = y_buf.shape[2]
    wide = t_ref.shape[1] // n
    part = wide // chunks
    barrier = pltpu.get_barrier_semaphore()
    for d in range(1, n):
        pl.semaphore_signal(barrier, inc=1, device_id=(lax.rem(gx + d, n), gy), device_id_type=MESH)
    pl.semaphore_wait(barrier, n - 1)

    first, second, local = [], [], []
    for m in range(chunks):
        for d in range(1, n):
            to = lax.rem(gx + d, n)
            lanes = pl.ds(pl.multiple_of(to * wide + m * part, 128), part)
            first.append(
                remote(t_ref.at[:, lanes], x_buf.at[m, gx], s1.at[m, d], r1.at[m, d], (to, gy))
            )
        lanes = pl.ds(pl.multiple_of(gx * wide + m * part, 128), part)
        own = pltpu.make_async_copy(t_ref.at[:, lanes], x_buf.at[m, gx], ls.at[m, 0])
        own.start()
        local.append(own)
    sketch_parts(f_ref, east_ref, north_ref, up_ref, q_ref, py_ref, px_buf)
    for m in range(chunks):
        local[m].wait()
        for d in range(1, n):
            first[m * (n - 1) + d - 1].wait()
        block = x_buf[m].reshape(n * rows, part)
        lanes = pl.ds(pl.multiple_of(gx * wide + m * part, 128), part)
        for d in range(1, n + 1):
            to = lax.rem(gx + d, n)
            y_buf[m, d - 1] = jnp.dot(g_ref[to], block, preferred_element_type=F32).astype(BF)
            if d < n:
                second.append(
                    remote(
                        y_buf.at[m, d - 1], w_ref.at[:, lanes], s2.at[m, d], r2.at[m, d], (to, gy)
                    )
                )
            else:
                own = pltpu.make_async_copy(y_buf.at[m, d - 1], w_ref.at[:, lanes], ls.at[m, 1])
                own.start()
                second.append(own)
    for copy in second:
        copy.wait()


def mix_x(field, gauss, n, a_rows, cells, east, north, up, ny):
    rows, lanes = field.shape
    wide = lanes // n
    chunks = 3 if wide % 384 == 0 else 1
    dma = lambda *shape: pltpu.SemaphoreType.DMA(shape)
    return pl.pallas_call(
        functools.partial(mix_x_kernel, n, chunks),
        out_shape=(
            jax.ShapeDtypeStruct((a_rows, lanes), BF),
            jax.ShapeDtypeStruct((ny, (cells.shape[0] + cells.shape[2]) // ny, up.shape[1]), F32),
            jax.ShapeDtypeStruct(north.shape, F32),
        ),
        in_specs=[VMEM] * 6,
        out_specs=(VMEM, VMEM, VMEM),
        scratch_shapes=[
            pltpu.VMEM((chunks, n, rows, wide // chunks), BF),
            pltpu.VMEM((chunks, n, a_rows, wide // chunks), BF),
            pltpu.VMEM(east.shape, F32),
            dma(chunks, n), dma(chunks, n), dma(chunks, n), dma(chunks, n), dma(chunks, 2),
        ],
        compiler_params=pltpu.CompilerParams(collective_id=0, has_side_effects=True),
    )(field, gauss, cells, east, north, up)


def exchange_kernel(
    nx, ny, batches, per_c, w_ref, gt_ref, mask_ref, q_ref, py_ref,
    r_ref, fx_ref, fz_ref, pyo_ref,
    u_buf, q_in, q_all, y_in, z_in, z_own,
    us, ur, ul, qs, qr, ys, yr, zs, zr, gs, gr,
):
    gx, gy = lax.axis_index("gx"), lax.axis_index("gy")
    span = u_buf.shape[3]
    per = u_buf.shape[2]
    lanes = u_buf.shape[4]
    a_in = mask_ref.shape[0]
    deep = gt_ref.shape[1]
    x_rows = q_ref.shape[1] - z_in.shape[1]
    barrier = pltpu.get_barrier_semaphore()
    for d in range(1, ny):
        pl.semaphore_signal(barrier, inc=1, device_id=(gx, lax.rem(gy + d, ny)), device_id_type=MESH)
    for d in range(1, nx):
        pl.semaphore_signal(barrier, inc=1, device_id=(lax.rem(gx + d, nx), gy), device_id_type=MESH)
    pl.semaphore_wait(barrier, nx + ny - 2)

    small, ysmall, big = [], [], []
    for d in range(1, ny):
        to = lax.rem(gy + d, ny)
        small.append(remote(q_ref.at[to], q_in.at[d], qs.at[d], qr.at[d], (gx, to)))
    for d in range(1, nx):
        to = lax.rem(gx + d, nx)
        ysmall.append(remote(py_ref, y_in.at[d], ys.at[d], yr.at[d], (to, gy)))

    rows_b = per * span
    for b in range(batches):
        for d in range(1, ny + 1):
            to = lax.rem(gy + d, ny)
            for tile in range(lanes // 128):
                low = min(tile * 128 // per_c, a_in - 1)
                high = min((tile * 128 + 127) // per_c, a_in - 1)
                here = slice(tile * 128, tile * 128 + 128)
                weights = jnp.concatenate(
                    [gt_ref[to, :, here] * mask_ref[k : k + 1, here] for k in range(low, high + 1)], axis=0
                )
                left = w_ref[b * rows_b : (b + 1) * rows_b, low * deep : (high + 1) * deep]
                got = jnp.dot(left, weights, preferred_element_type=F32).astype(BF)
                u_buf[b, d - 1, :, :, here] = got.reshape(per, span, 128)
            target = r_ref.at[pl.ds(b * per, per), pl.ds(pl.multiple_of(gy * span, span), span), :]
            if d < ny:
                big.append(remote(u_buf.at[b, d - 1], target, us.at[b, d], ur.at[b, d], (gx, to)))
            else:
                own = pltpu.make_async_copy(u_buf.at[b, d - 1], target, ul.at[b])
                own.start()
                big.append(own)
        if b == 0:
            for copy in small:
                copy.wait()
            total = q_ref[gy]
            for d in range(1, ny):
                total = total + q_in[d]
            z_own[...] = total[x_rows:]
            zsmall = []
            for d in range(1, nx):
                to = lax.rem(gx + d, nx)
                zsmall.append(remote(z_own, z_in.at[d], zs.at[d], zr.at[d], (to, gy)))
            for copy in ysmall:
                copy.wait()
            y_in[0] = py_ref[...]
            y_total = jnp.zeros(py_ref.shape, F32)
            for g in range(nx):
                y_total = y_total + y_in[lax.rem(gx - g + nx, nx)]
            pyo_ref[...] = y_total
    for copy in zsmall:
        copy.wait()
    z_in[0] = z_own[...]
    z_total = jnp.zeros(z_own.shape, F32)
    for g in range(nx):
        z_total = z_total + z_in[lax.rem(gx - g + nx, nx)]
    q_all[gy, :x_rows] = total[:x_rows]
    q_all[gy, x_rows:] = z_total
    gathers = []
    for d in range(1, ny):
        to = lax.rem(gy + d, ny)
        gathers.append(remote(q_all.at[gy], q_all.at[gy], gs.at[d], gr.at[d], (gx, to)))
    for copy in gathers:
        copy.wait()
    z_rows = z_own.shape[0]
    for k in range(ny):
        fx_ref[k * x_rows : (k + 1) * x_rows] = q_all[k, :x_rows]
        fz_ref[k * z_rows : (k + 1) * z_rows] = q_all[k, x_rows:]
    for copy in big:
        copy.wait()


def line_kernel(
    nx, ny, batches, per_c, w_ref, gt_ref, mask_ref, q_ref, py_ref,
    r_ref, fx_ref, fz_ref, pyo_ref,
    w_in, u_buf, wt, q_in, q_all, y_in, z_in, z_own,
    ws, wr, us, ur, ul, qs, qr, ys, yr, zs, zr, gs, gr,
):
    gx, gy = lax.axis_index("gx"), lax.axis_index("gy")
    spot, core = gy // 2, gy % 2
    last = ny // 2 - 1
    middle = jnp.logical_and(spot > 0, spot < last)
    left_half = spot * 2 < last
    end = jnp.where(left_half, 0, last)
    near = jnp.where(left_half, 1, last - 1)
    _, _, _, per, span, lanes = u_buf.shape
    a_in = mask_ref.shape[0]
    deep = gt_ref.shape[1]
    x_rows = q_ref.shape[1] - z_in.shape[1]
    rows_b = per * span
    spots = (end, last - spot, last - end, spot)
    goals = (gy, 2 * spot + 1 - core, 2 * end, 2 * end + 1)
    barrier = pltpu.get_barrier_semaphore()
    for d in range(1, ny):
        pl.semaphore_signal(barrier, inc=1, device_id=(gx, lax.rem(gy + d, ny)), device_id_type=MESH)
    for d in range(1, nx):
        pl.semaphore_signal(barrier, inc=1, device_id=(lax.rem(gx + d, nx), gy), device_id_type=MESH)
    pl.semaphore_wait(barrier, nx + ny - 2)

    small, ysmall = [], []
    for d in range(1, ny):
        to = lax.rem(gy + d, ny)
        small.append(remote(q_ref.at[to], q_in.at[d], qs.at[d], qr.at[d], (gx, to)))
    for d in range(1, nx):
        to = lax.rem(gx + d, nx)
        ysmall.append(remote(py_ref, y_in.at[d], ys.at[d], yr.at[d], (to, gy)))

    def raw(src, slot, b, to_spot):
        return pltpu.make_async_remote_copy(
            src_ref=src, dst_ref=w_in.at[slot, b], send_sem=ws.at[slot, b], recv_sem=wr.at[slot, b],
            device_id=(gx, 2 * to_spot + core), device_id_type=MESH,
        )

    def rows_of(b):
        return w_ref.at[pl.ds(b * rows_b, rows_b), :]

    def place(b, origin):
        return r_ref.at[pl.ds(b * per, per), pl.ds(pl.multiple_of(origin * span, span), span), :]

    def block(kind, slot, b):
        source = 2 * spots[slot] + core
        if kind == 0:
            return pltpu.make_async_copy(u_buf.at[kind, slot, b], place(b, source), ul.at[slot, b])
        return pltpu.make_async_remote_copy(
            src_ref=u_buf.at[kind, slot, b], dst_ref=place(b, source),
            send_sem=us.at[kind, slot, b], recv_sem=ur.at[b, spots[slot], core],
            device_id=(gx, goals[kind]), device_id_type=MESH,
        )

    def arrived(b, at, side):
        pltpu.make_async_remote_copy(
            src_ref=u_buf.at[0, 0, b], dst_ref=place(b, 2 * at + side),
            send_sem=us.at[1, 0, b], recv_sem=ur.at[b, at, side],
            device_id=(gx, goals[1]), device_id_type=MESH,
        ).wait_recv()

    pieces, base = [], 0
    for tile in range(lanes // 128):
        low = min(tile * 128 // per_c, a_in - 1)
        high = min((tile * 128 + 127) // per_c, a_in - 1)
        pieces.append((tile, low, high, base))
        base += (high + 1 - low) * deep

    def weigh(kind):
        for tile, low, high, at in pieces:
            here = slice(tile * 128, tile * 128 + 128)
            for k in range(low, high + 1):
                wt[kind, at + (k - low) * deep : at + (k - low + 1) * deep] = (
                    gt_ref[goals[kind], :, here] * mask_ref[k : k + 1, here]
                )

    def mix(kind, slot, b, left):
        for tile, low, high, at in pieces:
            got = jnp.dot(
                left[:, low * deep : (high + 1) * deep],
                wt[kind, at : at + (high + 1 - low) * deep],
                preferred_element_type=F32,
            ).astype(BF)
            u_buf[kind, slot, b, :, :, tile * 128 : tile * 128 + 128] = got.reshape(per, span, 128)

    def own_blocks(kind):
        weigh(kind)
        for b in range(batches):
            mix(kind, 3, b, rows_of(b))
            block(kind, 3, b).start()

    @pl.when(middle)
    def _():
        for b in range(batches):
            raw(rows_of(b), 1, b, last - spot).start()
        for kind in (2, 3):
            own_blocks(kind)

    @pl.when(jnp.logical_not(middle))
    def _():
        for b in range(batches):
            raw(rows_of(b), 0, b, near).start()

    for kind in (1, 0):
        own_blocks(kind)

    for copy in small:
        copy.wait()
    total = q_ref[gy]
    for d in range(1, ny):
        total = total + q_in[d]
    z_own[...] = total[x_rows:]
    zsmall = []
    for d in range(1, nx):
        to = lax.rem(gx + d, nx)
        zsmall.append(remote(z_own, z_in.at[d], zs.at[d], zr.at[d], (to, gy)))
    for copy in ysmall:
        copy.wait()
    y_in[0] = py_ref[...]
    y_total = jnp.zeros(py_ref.shape, F32)
    for g in range(nx):
        y_total = y_total + y_in[lax.rem(gx - g + nx, nx)]
    pyo_ref[...] = y_total
    for copy in zsmall:
        copy.wait()
    z_in[0] = z_own[...]
    z_total = jnp.zeros(z_own.shape, F32)
    for g in range(nx):
        z_total = z_total + z_in[lax.rem(gx - g + nx, nx)]
    q_all[gy, :x_rows] = total[:x_rows]
    q_all[gy, x_rows:] = z_total
    gathers = []
    for d in range(1, ny):
        to = lax.rem(gy + d, ny)
        gathers.append(remote(q_all.at[gy], q_all.at[gy], gs.at[d], gr.at[d], (gx, to)))

    @pl.when(middle)
    def _():
        for b in range(batches):
            raw(rows_of(b), 0, b, near).wait_recv()
            raw(w_in.at[0, b], 2, b, last - spot).start()
            raw(rows_of(b), 1, b, last - spot).wait_recv()
            for kind, slot in ((2, 1), (3, 1), (1, 1), (1, 0), (0, 1), (0, 0)):
                mix(kind, slot, b, w_in.at[slot, b])
                block(kind, slot, b).start()
        for b in range(batches):
            raw(w_in.at[0, b], 2, b, last - spot).wait_recv()
            for kind in (2, 3, 1, 0):
                mix(kind, 2, b, w_in.at[2, b])
                block(kind, 2, b).start()
        for b in range(batches):
            raw(rows_of(b), 1, b, last - spot).wait_send()
            raw(w_in.at[0, b], 2, b, last - spot).wait_send()
            for slot in range(4):
                block(0, slot, b).wait()
                block(1, slot, b).wait_send()
                if slot:
                    block(2, slot, b).wait_send()
                    block(3, slot, b).wait_send()
                arrived(b, spots[slot], 1 - core)

    @pl.when(jnp.logical_not(middle))
    def _():
        for b in range(batches):
            raw(rows_of(b), 0, b, near).wait_send()
            block(0, 3, b).wait()
            block(1, 3, b).wait_send()
            arrived(b, spot, 1 - core)
            for d in range(1, ny // 2):
                for side in range(2):
                    arrived(b, lax.rem(spot + d, ny // 2), side)

    for copy in gathers:
        copy.wait()
    z_rows = z_own.shape[0]
    for k in range(ny):
        fx_ref[k * x_rows : (k + 1) * x_rows] = q_all[k, :x_rows]
        fz_ref[k * z_rows : (k + 1) * z_rows] = q_all[k, x_rows:]


def exchange(w, gt, mask, q, py, nx, ny, groups, span, per_c):
    lanes = gt.shape[2]
    deep = gt.shape[1]
    z_rows = deep // ny
    dma = lambda *shape: pltpu.SemaphoreType.DMA(shape)
    vm = pltpu.VMEM
    sums = [
        vm(q.shape, F32), vm(q.shape, F32), vm((nx,) + py.shape, F32),
        vm((nx, z_rows, q.shape[2]), F32), vm((z_rows, q.shape[2]), F32),
    ]
    sum_sems = [dma(ny), dma(ny), dma(nx), dma(nx), dma(nx), dma(nx), dma(ny), dma(ny)]
    if ny == 8 and groups % 4 == 0:
        batches = 4
        per = groups // batches
        total_k = sum(
            min((t * 128 + 127) // per_c, mask.shape[0] - 1) + 1 - t * 128 // per_c
            for t in range(lanes // 128)
        ) * deep
        body = functools.partial(line_kernel, nx, ny, batches, per_c)
        scratch = [
            vm((3, batches, per * span, w.shape[1]), BF),
            vm((4, 4, batches, per, span, lanes), BF),
            vm((4, total_k, 128), BF),
        ] + sums + [
            dma(3, batches), dma(3, batches), dma(4, 4, batches), dma(batches, ny // 2, 2),
            dma(4, batches),
        ] + sum_sems
    else:
        batches = 3 if groups % 3 == 0 else 1
        per = groups // batches
        body = functools.partial(exchange_kernel, nx, ny, batches, per_c)
        scratch = [vm((batches, ny, per, span, lanes), BF)] + sums + [
            dma(batches, ny), dma(batches, ny), dma(batches)
        ] + sum_sems
    return pl.pallas_call(
        body,
        out_shape=(
            jax.ShapeDtypeStruct((groups, ny * span, lanes), BF),
            jax.ShapeDtypeStruct((ny * q.shape[1] - deep, q.shape[2]), F32),
            jax.ShapeDtypeStruct((deep, q.shape[2]), F32),
            jax.ShapeDtypeStruct(py.shape, F32),
        ),
        in_specs=[VMEM] * 5,
        out_specs=(ANY, VMEM, VMEM, VMEM),
        scratch_shapes=scratch,
        compiler_params=pltpu.CompilerParams(collective_id=1, has_side_effects=True),
    )(w, gt, mask, q, py)


def flow_kernel(
    nx, ny, per_c, ft_ref, g_ref, gu_ref, sel_ref, mask_ref, east_ref, north_ref, up_ref,
    r_ref, fx_ref, fz_ref, fy_ref,
    f_buf, x_buf, y_buf, w_land, wf, w_own, w_in, u_buf, wt,
    q_buf, q_in, q_all, p_buf, y_in, z_in, z_own,
    s1, r1, l1, s2, r2, ws, wr, us, ur, ul, fs, qs, qr, ys, yr, zs, zr, gs, gr,
):
    gx, gy = lax.axis_index("gx"), lax.axis_index("gy")
    spot, core = gy // 2, gy % 2
    last = ny // 2 - 1
    middle = jnp.logical_and(spot > 0, spot < last)
    left_half = spot * 2 < last
    end = jnp.where(left_half, 0, last)
    near = jnp.where(left_half, 1, last - 1)
    spots = (end, last - spot, last - end, spot)
    goals = (gy, 2 * spot + 1 - core, 2 * end, 2 * end + 1)

    span, rows, deep = f_buf.shape
    steps, share = x_buf.shape[:2]
    _, _, _, groups, tall, lanes = u_buf.shape
    a_in = mask_ref.shape[0]
    a_rows = groups * a_in
    width = up_ref.shape[1]
    x_rows, z_rows = rows // ny, deep // ny

    load = pltpu.make_async_copy(ft_ref, f_buf, fs.at[0])
    load.start()
    barrier = pltpu.get_barrier_semaphore()
    for d in range(1, ny):
        pl.semaphore_signal(barrier, inc=1, device_id=(gx, lax.rem(gy + d, ny)), device_id_type=MESH)
    for d in range(1, nx):
        pl.semaphore_signal(barrier, inc=1, device_id=(lax.rem(gx + d, nx), gy), device_id_type=MESH)
    pl.semaphore_wait(barrier, nx + ny - 2)

    def send(src, dst, ssem, rsem, where):
        return pltpu.make_async_remote_copy(
            src_ref=src, dst_ref=dst, send_sem=ssem, recv_sem=rsem, device_id=where, device_id_type=MESH
        )

    def first(m, d):
        to = lax.rem(gx + d, nx)
        src = ft_ref.at[pl.ds(m * tall + to * share, share)]
        dst = x_buf.at[m, :, pl.ds(pl.multiple_of(gx * rows, rows), rows), :]
        if d == nx:
            return pltpu.make_async_copy(src, dst, l1.at[m])
        return send(src, dst, s1.at[m, d], r1.at[m, d], (to, gy))

    def second(m, d):
        to = lax.rem(gx + d, nx)
        return send(y_buf.at[m, d - 1], w_land.at[m, gx], s2.at[m, d], r2.at[m, d], (to, gy))

    def send_first(m):
        for d in range(1, nx + 1):
            first(m, d).start()

    def mix_first(m):
        first(m, nx).wait()
        for d in range(1, nx):
            first(m, d).wait_recv()
        block = jnp.concatenate([x_buf[m, j] for j in range(share)], axis=1)
        for d in range(1, nx + 1):
            to = lax.rem(gx + d, nx)
            got = jnp.dot(g_ref[to], block, preferred_element_type=F32).astype(BF)
            if d < nx:
                y_buf[m, d - 1] = got
                second(m, d).start()
            else:
                w_land[m, gx] = got

    def raw(src, slot, m, to_spot):
        return send(src, w_in.at[slot, m], ws.at[slot, m], wr.at[slot, m], (gx, 2 * to_spot + core))

    def place(m, origin):
        return r_ref.at[:, pl.ds(pl.multiple_of(origin * span + m * tall, tall), tall), :]

    def block(kind, slot, m):
        source = 2 * spots[slot] + core
        if kind == 0:
            return pltpu.make_async_copy(u_buf.at[kind, slot, m], place(m, source), ul.at[slot, m])
        return send(
            u_buf.at[kind, slot, m], place(m, source), us.at[kind, slot, m],
            ur.at[m, spots[slot], core], (gx, goals[kind]),
        )

    def arrived(m, at, side):
        send(
            u_buf.at[0, 0, m], place(m, 2 * at + side), us.at[1, 0, m], ur.at[m, at, side], (gx, goals[1])
        ).wait_recv()

    pieces, base = [], 0
    for tile in range(lanes // 128):
        low = min(tile * 128 // per_c, a_in - 1)
        high = min((tile * 128 + 127) // per_c, a_in - 1)
        pieces.append((tile, low, high, base))
        base += (high + 1 - low) * deep

    def weigh(kind):
        mine = gu_ref[pl.ds(pl.multiple_of(goals[kind] * per_c, per_c), per_c), :]
        spread = lax.dot_general(
            mine, sel_ref[...], (((0,), (0,)), ((), ())), preferred_element_type=F32
        )
        for tile, low, high, at in pieces:
            here = slice(tile * 128, tile * 128 + 128)
            for k in range(low, high + 1):
                wt[kind, at + (k - low) * deep : at + (k - low + 1) * deep] = (
                    spread[:, here] * mask_ref[k : k + 1, here]
                ).astype(BF)

    def mix(kind, slot, m, left):
        for tile, low, high, at in pieces:
            got = jnp.dot(
                left[:, low * deep : (high + 1) * deep],
                wt[kind, at : at + (high + 1 - low) * deep],
                preferred_element_type=F32,
            )
            u_buf[kind, slot, m, :, :, tile * 128 : tile * 128 + 128] = (
                got.reshape(groups, tall, 128).astype(BF)
            )
        block(kind, slot, m).start()

    def settle(m):
        for d in range(1, nx):
            second(m, d).wait_recv()
        for y in range(tall):
            at = (y % share) * deep
            wf[pl.ds(y, a_rows, stride=tall), :] = w_land[m, y // share, :, at : at + deep].astype(F32)
        for k in range(a_in):
            part = jnp.concatenate(
                [wf[(g * a_in + k) * tall : (g * a_in + k + 1) * tall, :] for g in range(groups)], axis=0
            )
            w_own[m, :, k * deep : (k + 1) * deep] = part.astype(BF)

    def sketch():
        step = 16 if span % 16 == 0 else span
        along_x = east_ref[...].astype(F32)[None]
        part_x = jnp.zeros((rows, width), F32)
        part_z = jnp.zeros((deep, width), F32)
        for c in range(0, span, step):
            cells = f_buf[c : c + step].reshape(step * rows, deep)
            along_y = north_ref[c : c + step].astype(F32)[:, None, :]
            weighted = jnp.dot(cells, up_ref[...], preferred_element_type=F32).reshape(step, rows, width)
            p_buf[c : c + step] = jnp.sum(weighted * along_x, axis=1)
            part_x = part_x + jnp.sum(weighted * along_y, axis=0)
            khatri = (along_x * along_y).astype(BF).reshape(step * rows, width)
            part_z = part_z + lax.dot_general(
                cells, khatri, (((0,), (0,)), ((), ())), preferred_element_type=F32
            )
        for k in range(ny):
            q_buf[k, :x_rows] = part_x[k * x_rows : (k + 1) * x_rows]
            q_buf[k, x_rows:] = part_z[k * z_rows : (k + 1) * z_rows]

    def small(d):
        to = lax.rem(gy + d, ny)
        return send(q_buf.at[to], q_in.at[d], qs.at[d], qr.at[d], (gx, to))

    def small_y(d):
        to = lax.rem(gx + d, nx)
        return send(p_buf, y_in.at[d], ys.at[d], yr.at[d], (to, gy))

    def small_z(d):
        to = lax.rem(gx + d, nx)
        return send(z_own, z_in.at[d], zs.at[d], zr.at[d], (to, gy))

    def gather(d):
        to = lax.rem(gy + d, ny)
        return send(q_all.at[gy], q_all.at[gy], gs.at[d], gr.at[d], (gx, to))

    def gathered(d):
        source = lax.rem(gy - d + ny, ny)
        return send(q_all.at[source], q_all.at[source], gs.at[d], gr.at[d], (gx, source))

    send_first(0)
    send_first(1)
    load.wait()
    sketch()
    for d in range(1, ny):
        small(d).start()
    for d in range(1, nx):
        small_y(d).start()
    mix_first(0)
    send_first(2)
    for kind in range(4):
        weigh(kind)

    def stage(s, carry):
        @pl.when(s + 1 < steps)
        def _():
            mix_first(s + 1)

        @pl.when(s + 3 < steps)
        def _():
            send_first(s + 3)

        @pl.when(s < steps)
        def _():
            settle(s)

        @pl.when(jnp.logical_and(s < steps, middle))
        def _():
            raw(w_own.at[s], 1, s, last - spot).start()
            for kind in (2, 3):
                mix(kind, 3, s, w_own.at[s])

        @pl.when(jnp.logical_and(s < steps, jnp.logical_not(middle)))
        def _():
            raw(w_own.at[s], 0, s, near).start()

        @pl.when(s < steps)
        def _():
            for kind in (1, 0):
                mix(kind, 3, s, w_own.at[s])

        @pl.when(jnp.logical_and(jnp.logical_and(s >= 1, s < steps + 1), middle))
        def _():
            m = s - 1
            raw(w_own.at[m], 0, m, near).wait_recv()
            raw(w_in.at[0, m], 2, m, last - spot).start()
            raw(w_own.at[m], 1, m, last - spot).wait_recv()
            for kind, slot in ((2, 1), (3, 1), (1, 1), (0, 1), (1, 0), (0, 0)):
                mix(kind, slot, m, w_in.at[slot, m])

        @pl.when(jnp.logical_and(s >= 2, middle))
        def _():
            m = s - 2
            raw(w_in.at[0, m], 2, m, last - spot).wait_recv()
            for kind in (2, 3, 1, 0):
                mix(kind, 2, m, w_in.at[2, m])

        @pl.when(s == 1)
        def _():
            for d in range(1, ny):
                small(d).wait()
            total = q_buf[gy]
            for d in range(1, ny):
                total = total + q_in[d]
            q_all[gy] = total
            z_own[...] = total[x_rows:]
            for d in range(1, nx):
                small_z(d).start()

        @pl.when(s == 3)
        def _():
            for d in range(1, nx):
                small_y(d).wait()
                small_z(d).wait()
            y_in[0] = p_buf[...]
            z_in[0] = z_own[...]
            y_total = jnp.zeros(p_buf.shape, F32)
            z_total = jnp.zeros(z_own.shape, F32)
            for g in range(nx):
                y_total = y_total + y_in[lax.rem(gx - g + nx, nx)]
                z_total = z_total + z_in[lax.rem(gx - g + nx, nx)]
            fy_ref[...] = y_total
            q_all[gy, x_rows:] = z_total
            for d in range(1, ny):
                gather(d).start()

        return carry

    lax.fori_loop(0, steps + 2, stage, 0)

    for d in range(1, ny):
        gather(d).wait_send()
        gathered(d).wait_recv()
    for k in range(ny):
        fx_ref[k * x_rows : (k + 1) * x_rows] = q_all[k, :x_rows]
        fz_ref[k * z_rows : (k + 1) * z_rows] = q_all[k, x_rows:]

    def close(m, carry):
        for d in range(1, nx):
            first(m, d).wait_send()
            second(m, d).wait_send()
        block(0, 3, m).wait()
        block(1, 3, m).wait_send()
        arrived(m, spot, 1 - core)

        @pl.when(middle)
        def _():
            raw(w_own.at[m], 1, m, last - spot).wait_send()
            raw(w_in.at[0, m], 2, m, last - spot).wait_send()
            block(2, 3, m).wait_send()
            block(3, 3, m).wait_send()
            for slot in range(3):
                block(0, slot, m).wait()
                block(1, slot, m).wait_send()
                if slot:
                    block(2, slot, m).wait_send()
                    block(3, slot, m).wait_send()
                arrived(m, spots[slot], 1 - core)

        @pl.when(jnp.logical_not(middle))
        def _():
            raw(w_own.at[m], 0, m, near).wait_send()
            for d in range(1, ny // 2):
                for side in range(2):
                    arrived(m, lax.rem(spot + d, ny // 2), side)

        return carry

    lax.fori_loop(0, steps, close, 0)


def flow(field, gauss_east, gauss_up, east, north, up, nx, ny, a_in, lanes):
    rows, span, deep = field.shape
    a_rows = gauss_east.shape[0] // nx
    per_c = gauss_up.shape[0] // ny
    groups = a_rows // a_in
    tall = 8
    steps, share = span // tall, tall // nx
    width = up.shape[1]
    x_rows, z_rows = rows // ny, deep // ny
    lane = np.arange(lanes)
    used = lane < a_in * per_c
    sel = np.logical_and(lane[None] % per_c == np.arange(per_c)[:, None], used[None]).astype(np.float32)
    mask = (lane[None] // per_c == np.arange(a_in)[:, None]).astype(np.float32)
    total_k = sum(
        min((t * 128 + 127) // per_c, a_in - 1) + 1 - min(t * 128 // per_c, a_in - 1)
        for t in range(lanes // 128)
    ) * deep
    dma = lambda *shape: pltpu.SemaphoreType.DMA(shape)
    vm = pltpu.VMEM
    q_shape = (ny, x_rows + z_rows, width)
    scratch = [
        vm((span, rows, deep), BF),
        vm((steps, share, nx * rows, deep), BF),
        vm((steps, nx - 1, a_rows, share * deep), BF),
        vm((steps, nx, a_rows, share * deep), BF),
        vm((a_rows * tall, deep), F32),
        vm((steps, groups * tall, a_in * deep), BF),
        vm((3, steps, groups * tall, a_in * deep), BF),
        vm((4, 4, steps, groups, tall, lanes), BF),
        vm((4, total_k, 128), BF),
        vm(q_shape, F32), vm(q_shape, F32), vm(q_shape, F32),
        vm((span, width), F32), vm((nx, span, width), F32),
        vm((nx, z_rows, width), F32), vm((z_rows, width), F32),
        dma(steps, nx), dma(steps, nx), dma(steps), dma(steps, nx), dma(steps, nx),
        dma(3, steps), dma(3, steps), dma(4, 4, steps), dma(steps, ny // 2, 2), dma(4, steps), dma(1),
        dma(ny), dma(ny), dma(nx), dma(nx), dma(nx), dma(nx), dma(ny), dma(ny),
    ]
    return pl.pallas_call(
        functools.partial(flow_kernel, nx, ny, per_c),
        out_shape=(
            jax.ShapeDtypeStruct((groups, ny * span, lanes), BF),
            jax.ShapeDtypeStruct((rows, width), F32),
            jax.ShapeDtypeStruct((deep, width), F32),
            jax.ShapeDtypeStruct((span, width), F32),
        ),
        in_specs=[ANY] + [VMEM] * 7,
        out_specs=(ANY, VMEM, VMEM, VMEM),
        scratch_shapes=scratch,
        compiler_params=pltpu.CompilerParams(collective_id=2, has_side_effects=True),
    )(
        field.transpose(1, 0, 2), gauss_east.reshape(nx, a_rows, -1), gauss_up,
        jnp.asarray(sel, BF), jnp.asarray(mask, F32), east, north, up,
    )


def mix_y_kernel(r_ref, g_ref, o_ref):
    for k in range(r_ref.shape[0]):
        o_ref[k] = lax.dot_general(
            r_ref[k], g_ref[...], (((0,), (1,)), ((), ())), preferred_element_type=F32
        )


def mix_y(r, g):
    groups, deep, lanes = r.shape
    out = g.shape[0]
    take = 2 if groups % 2 == 0 else 1
    return pl.pallas_call(
        mix_y_kernel,
        grid=(groups // take,),
        out_shape=jax.ShapeDtypeStruct((groups, lanes, out), F32),
        in_specs=[
            pl.BlockSpec((take, deep, lanes), lambda i: (i, 0, 0)),
            pl.BlockSpec((out, deep), lambda i: (0, 0)),
        ],
        out_specs=pl.BlockSpec((take, lanes, out), lambda i: (i, 0, 0)),
    )(r, g)


def per_device(
    nx, ny,
    thermal_field,
    probe_range_east,
    probe_range_north,
    probe_range_upward,
    gauss_kernel_east,
    gauss_kernel_north,
    gauss_kernel_upward,
):
    rows, span, deep = thermal_field.shape
    a_rows = gauss_kernel_east.shape[0] // nx
    per_c = gauss_kernel_upward.shape[0] // ny
    a_in = 8 if a_rows % 8 == 0 and 8 * per_c % 128 == 0 else a_rows
    groups = a_rows // a_in
    used = a_in * per_c
    lanes = -(-used // 128) * 128

    if ny == 8 and 8 % nx == 0 and span % 8 == 0 and span // 8 > 2 and a_in % 8 == 0 and per_c % 16 == 0:
        r, factor_x, factor_z, factor_y = flow(
            thermal_field, gauss_kernel_east, gauss_kernel_upward,
            probe_range_east, probe_range_north, probe_range_upward, nx, ny, a_in, lanes,
        )
    else:
        w, q, part_y = mix_x(
            thermal_field.reshape(rows, span * deep),
            gauss_kernel_east.reshape(nx, a_rows, -1),
            nx,
            a_rows,
            thermal_field,
            probe_range_east,
            probe_range_north,
            probe_range_upward,
            ny,
        )
        w = w.reshape(groups, a_in, span, deep).transpose(0, 2, 1, 3).reshape(groups * span, a_in * deep)

        gt = gauss_kernel_upward.reshape(ny, per_c, deep).transpose(0, 2, 1)
        gt = jnp.pad(jnp.tile(gt, (1, 1, a_in)), ((0, 0), (0, 0), (0, lanes - used)))
        mask = (
            lax.broadcasted_iota(jnp.int32, (a_in, lanes), 1) // per_c
            == lax.broadcasted_iota(jnp.int32, (a_in, lanes), 0)
        ).astype(BF)
        r, factor_x, factor_z, factor_y = exchange(w, gt, mask, q, part_y, nx, ny, groups, span, per_c)

    core = mix_y(r, gauss_kernel_north)
    core = core[:, :used].reshape(a_rows, per_c, -1).transpose(0, 2, 1)
    return (factor_x, factor_y, factor_z, core)


def solution(mesh):
    in_specs = (P("gx", "gy", None), P("gx", None), P("gy", None), P(), P(), P(), P())
    out_specs = (P("gx", None), P("gy", None), P(), P("gx", None, "gy"))
    body = functools.partial(per_device, mesh.shape["gx"], mesh.shape["gy"])
    return jax.shard_map(
        body, mesh=mesh, in_specs=in_specs, out_specs=out_specs, check_vma=False
    )
```

profile of v0, /device:TPU:1, one launch (start us, length us, event | category | flops | bytes accessed | tf_op | source)
XLA Modules:
  0.0 93.0 jit_solution(993180070588480782)
XLA Ops:
  0.6 2.6 %copy.15 = bf16[96,48,128]{2,0,1:T(8,128)(2,1)} copy(bf16[96,48,128]{2,1,0:T(8,128)(2,1)} %param.9) | data formatting | bytes 2359296 | tf_op args[0]
  3.2 80.3 %shard_map.120 = (bf16[12,384,384]{2,1,0:T(8,128)(2,1)}, f32[96,128]{1,0:T(8,128)}, f32[128,128]{1,0:T(8,128)}, f32[48,128]{1,0:T(8,128)}) custom-call(bf16[48,96,128]{2,1,0:T(8,128)(2,1)} %bitcast.8, bf16[4,96,384]{2,1,0:T(8,128)(2,1)} %bitcast.9, bf16[384,128]{1,0:T(8,128)(2,1)} %gu_ref.1, bf16[48,384]{1,0:T(8,128)(2,1)} %constant.4.clone.sel_ref, ...), custom_call_target="tpu_custom_call" | custom-call | tf_op jit(solution)/shard_map/pallas_call | solution.py:785
  83.6 0.0 copy-start.1
  83.6 0.0 copy-start.2
  83.6 0.0 copy-start
  83.6 7.5 %shard_map.121 = f32[12,384,384]{2,1,0:T(8,128)} custom-call(bf16[12,384,384]{2,1,0:T(8,128)(2,1)} %get-tuple-element.11.r_ref, bf16[384,384]{1,0:T(8,128)(2,1)} %g_ref.1), custom_call_target="tpu_custom_call" | custom-call | tf_op jit(solution)/shard_map/pallas_call | solution.py:814
  91.1 0.0 copy-done.1
  91.1 0.6 copy.19
  91.7 0.0 copy-done.2
  91.7 0.6 copy.20
  92.4 0.0 copy-done
  92.4 0.6 copy.21
Async XLA Ops:
  83.6 7.6 %copy-start.1 = (f32[96,128]{1,0:T(8,128)S(1)}, f32[96,128]{1,0:T(8,128)}, u32[]{:S(2)}) copy-start(f32[96,128]{1,0:T(8,128)} %get-tuple-element.16) | copy-start | bytes 147460
  83.6 8.2 %copy-start.2 = (f32[48,128]{1,0:T(8,128)S(1)}, f32[48,128]{1,0:T(8,128)}, u32[]{:S(2)}) copy-start(f32[48,128]{1,0:T(8,128)} %get-tuple-element.17) | copy-start | bytes 73732
  83.6 8.8 %copy-start = (f32[128,128]{1,0:T(8,128)S(1)}, f32[128,128]{1,0:T(8,128)}, u32[]{:S(2)}) copy-start(f32[128,128]{1,0:T(8,128)} %get-tuple-element.18) | copy-start | bytes 196612
where the time goes:
time: 93.3 us; the launch traced here: 93 us
  Pallas kernels  87.9 us (94%)
  local copies, waits for them, and re-layouts  4.46 us (5%)
    pallas_call x1, Pallas kernels, flow(): pl.pallas_call(functools.partial(flow_kernel, nx, ny, per_c), out_shape=(...  80.3 us
    pallas_call x1, Pallas kernels, mix_y(): pl.pallas_call(mix_y_kernel, grid=(groups // take,), out_shape=jax.ShapeD...  7.54 us
    unnamed x10, local copies, waits for them, and re-layouts  4.46 us

commit v1 on v0

--- a/solution.py
+++ b/solution.py
@@ -444,11 +444,12 @@
 
 
 def flow_kernel(
-    nx, ny, per_c, ft_ref, g_ref, gu_ref, sel_ref, mask_ref, east_ref, north_ref, up_ref,
-    r_ref, fx_ref, fz_ref, fy_ref,
-    f_buf, x_buf, y_buf, w_land, wf, w_own, w_in, u_buf, wt,
+    nx, ny, per_c, field, gauss, gauss_up, select, masks, east, north, up,
+    r_ref, fx_out, fz_out, fy_out,
+    g_ref, gu_ref, sel_ref, mask_ref, east_ref, north_ref, up_ref, fx_ref, fz_ref, fy_ref,
+    n_buf, t_buf, f_buf, x_buf, y_buf, w_land, wf, w_own, w_in, u_buf, wt,
     q_buf, q_in, q_all, p_buf, y_in, z_in, z_own,
-    s1, r1, l1, s2, r2, ws, wr, us, ur, ul, fs, qs, qr, ys, yr, zs, zr, gs, gr,
+    s1, r1, l1, s2, r2, ws, wr, us, ur, ul, fs, os, ds, qs, qr, ys, yr, zs, zr, gs, gr,
 ):
     gx, gy = lax.axis_index("gx"), lax.axis_index("gy")
     spot, core = gy // 2, gy % 2
@@ -468,8 +469,24 @@
     width = up_ref.shape[1]
     x_rows, z_rows = rows // ny, deep // ny
 
-    load = pltpu.make_async_copy(ft_ref, f_buf, fs.at[0])
-    load.start()
+    batch = n_buf.shape[2]
+    loads = [
+        pltpu.make_async_copy(field.at[:, c * batch : (c + 1) * batch, :], n_buf.at[c], fs.at[c])
+        for c in range(span // batch)
+    ]
+    for copy in loads:
+        copy.start()
+    small_loads = [
+        pltpu.make_async_copy(src, dst, os.at[k])
+        for k, (src, dst) in enumerate(
+            (
+                (east, east_ref), (north, north_ref), (up, up_ref), (gauss, g_ref),
+                (gauss_up, gu_ref), (select, sel_ref), (masks, mask_ref),
+            )
+        )
+    ]
+    for copy in small_loads:
+        copy.start()
     barrier = pltpu.get_barrier_semaphore()
     for d in range(1, ny):
         pl.semaphore_signal(barrier, inc=1, device_id=(gx, lax.rem(gy + d, ny)), device_id_type=MESH)
@@ -484,7 +501,7 @@
 
     def first(m, d):
         to = lax.rem(gx + d, nx)
-        src = ft_ref.at[pl.ds(m * tall + to * share, share)]
+        src = f_buf.at[pl.ds(m * tall + to * share, share)]
         dst = x_buf.at[m, :, pl.ds(pl.multiple_of(gx * rows, rows), rows), :]
         if d == nx:
             return pltpu.make_async_copy(src, dst, l1.at[m])
@@ -614,9 +631,19 @@
         source = lax.rem(gy - d + ny, ny)
         return send(q_all.at[source], q_all.at[source], gs.at[d], gr.at[d], (gx, source))
 
+    def turn(c):
+        loads[c].wait()
+        t_buf[...] = n_buf[c].astype(F32).reshape(rows * batch, deep)
+        for y in range(batch):
+            f_buf[c * batch + y] = t_buf[pl.ds(y, rows, stride=batch), :].astype(BF)
+
+    turn(0)
     send_first(0)
     send_first(1)
-    load.wait()
+    for c in range(1, span // batch):
+        turn(c)
+    for copy in small_loads:
+        copy.wait()
     sketch()
     for d in range(1, ny):
         small(d).start()
@@ -626,6 +653,8 @@
     send_first(2)
     for kind in range(4):
         weigh(kind)
+
+    done_y = pltpu.make_async_copy(fy_ref, fy_out, ds.at[0])
 
     def stage(s, carry):
         @pl.when(s + 1 < steps)
@@ -696,6 +725,7 @@
                 y_total = y_total + y_in[lax.rem(gx - g + nx, nx)]
                 z_total = z_total + z_in[lax.rem(gx - g + nx, nx)]
             fy_ref[...] = y_total
+            done_y.start()
             q_all[gy, x_rows:] = z_total
             for d in range(1, ny):
                 gather(d).start()
@@ -710,6 +740,10 @@
     for k in range(ny):
         fx_ref[k * x_rows : (k + 1) * x_rows] = q_all[k, :x_rows]
         fz_ref[k * z_rows : (k + 1) * z_rows] = q_all[k, x_rows:]
+    done_x = pltpu.make_async_copy(fx_ref, fx_out, ds.at[1])
+    done_z = pltpu.make_async_copy(fz_ref, fz_out, ds.at[2])
+    done_x.start()
+    done_z.start()
 
     def close(m, carry):
         for d in range(1, nx):
@@ -743,6 +777,8 @@
         return carry
 
     lax.fori_loop(0, steps, close, 0)
+    for copy in (done_x, done_y, done_z):
+        copy.wait()
 
 
 def flow(field, gauss_east, gauss_up, east, north, up, nx, ny, a_in, lanes):
@@ -765,7 +801,13 @@
     dma = lambda *shape: pltpu.SemaphoreType.DMA(shape)
     vm = pltpu.VMEM
     q_shape = (ny, x_rows + z_rows, width)
+    batch = 16 if span % 16 == 0 else tall
     scratch = [
+        vm((nx, a_rows, gauss_east.shape[1]), BF), vm(gauss_up.shape, BF), vm(sel.shape, BF),
+        vm(mask.shape, F32), vm(east.shape, BF), vm(north.shape, BF), vm(up.shape, BF),
+        vm((rows, width), F32), vm((deep, width), F32), vm((span, width), F32),
+        vm((span // batch, rows, batch, deep), BF),
+        vm((rows * batch, deep), F32),
         vm((span, rows, deep), BF),
         vm((steps, share, nx * rows, deep), BF),
         vm((steps, nx - 1, a_rows, share * deep), BF),
@@ -779,48 +821,76 @@
         vm((span, width), F32), vm((nx, span, width), F32),
         vm((nx, z_rows, width), F32), vm((z_rows, width), F32),
         dma(steps, nx), dma(steps, nx), dma(steps), dma(steps, nx), dma(steps, nx),
-        dma(3, steps), dma(3, steps), dma(4, 4, steps), dma(steps, ny // 2, 2), dma(4, steps), dma(1),
+        dma(3, steps), dma(3, steps), dma(4, 4, steps), dma(steps, ny // 2, 2), dma(4, steps),
+        dma(span // batch), dma(7), dma(3),
         dma(ny), dma(ny), dma(nx), dma(nx), dma(nx), dma(nx), dma(ny), dma(ny),
     ]
     return pl.pallas_call(
         functools.partial(flow_kernel, nx, ny, per_c),
         out_shape=(
-            jax.ShapeDtypeStruct((groups, ny * span, lanes), BF),
+            pltpu.VMEM((groups, ny * span, lanes), BF),
             jax.ShapeDtypeStruct((rows, width), F32),
             jax.ShapeDtypeStruct((deep, width), F32),
             jax.ShapeDtypeStruct((span, width), F32),
         ),
-        in_specs=[ANY] + [VMEM] * 7,
-        out_specs=(ANY, VMEM, VMEM, VMEM),
+        in_specs=[ANY] * 8,
+        out_specs=(VMEM, ANY, ANY, ANY),
         scratch_shapes=scratch,
         compiler_params=pltpu.CompilerParams(collective_id=2, has_side_effects=True),
     )(
-        field.transpose(1, 0, 2), gauss_east.reshape(nx, a_rows, -1), gauss_up,
+        field, gauss_east.reshape(nx, a_rows, -1), gauss_up,
         jnp.asarray(sel, BF), jnp.asarray(mask, F32), east, north, up,
     )
 
 
-def mix_y_kernel(r_ref, g_ref, o_ref):
-    for k in range(r_ref.shape[0]):
-        o_ref[k] = lax.dot_general(
-            r_ref[k], g_ref[...], (((0,), (1,)), ((), ())), preferred_element_type=F32
+def mix_y_kernel(
+    take, r_ref, g_ref, fx_ref, fy_ref, fz_ref, o_ref, fx_out, fy_out, fz_out,
+    g_buf, o_buf, fx_buf, fy_buf, fz_buf, gs, os, fs, ts,
+):
+    groups = o_buf.shape[0]
+    load = pltpu.make_async_copy(g_ref, g_buf, gs.at[0])
+    load.start()
+    trios = ((fx_ref, fx_buf, fx_out), (fy_ref, fy_buf, fy_out), (fz_ref, fz_buf, fz_out))
+    ins = [pltpu.make_async_copy(src, mid, fs.at[k]) for k, (src, mid, _) in enumerate(trios)]
+    stores = [pltpu.make_async_copy(mid, dst, ts.at[k]) for k, (_, mid, dst) in enumerate(trios)]
+    for copy in ins:
+        copy.start()
+    load.wait()
+    for c in range(0, groups, take):
+        for k in range(c, c + take):
+            o_buf[k] = lax.dot_general(
+                r_ref[k], g_buf[...], (((0,), (1,)), ((), ())), preferred_element_type=F32
+            )
+        store = pltpu.make_async_copy(
+            o_buf.at[pl.ds(c, take)], o_ref.at[pl.ds(c, take)], os.at[c // take]
         )
-
-
-def mix_y(r, g):
+        store.start()
+        stores.append(store)
+        if c == 0:
+            for k in range(3):
+                ins[k].wait()
+                stores[k].start()
+    for copy in stores:
+        copy.wait()
+
+
+def mix_y(r, g, fx, fy, fz):
     groups, deep, lanes = r.shape
     out = g.shape[0]
-    take = 2 if groups % 2 == 0 else 1
+    take = 1 if groups % 1 == 0 else 1
+    dma = lambda *shape: pltpu.SemaphoreType.DMA(shape)
+    vm = pltpu.VMEM
+    like = lambda x: jax.ShapeDtypeStruct(x.shape, x.dtype)
     return pl.pallas_call(
-        mix_y_kernel,
-        grid=(groups // take,),
-        out_shape=jax.ShapeDtypeStruct((groups, lanes, out), F32),
-        in_specs=[
-            pl.BlockSpec((take, deep, lanes), lambda i: (i, 0, 0)),
-            pl.BlockSpec((out, deep), lambda i: (0, 0)),
+        functools.partial(mix_y_kernel, take),
+        out_shape=(jax.ShapeDtypeStruct((groups, lanes, out), F32), like(fx), like(fy), like(fz)),
+        in_specs=[VMEM, ANY, ANY, ANY, ANY],
+        out_specs=(ANY, ANY, ANY, ANY),
+        scratch_shapes=[
+            vm(g.shape, BF), vm((groups, lanes, out), F32), vm(fx.shape, F32), vm(fy.shape, F32),
+            vm(fz.shape, F32), dma(1), dma(groups // take), dma(3), dma(3),
         ],
-        out_specs=pl.BlockSpec((take, lanes, out), lambda i: (i, 0, 0)),
-    )(r, g)
+    )(r, g, fx, fy, fz)
 
 
 def per_device(
@@ -846,6 +916,7 @@
             thermal_field, gauss_kernel_east, gauss_kernel_upward,
             probe_range_east, probe_range_north, probe_range_upward, nx, ny, a_in, lanes,
         )
+        r = pltpu.with_memory_space_constraint(r, pltpu.VMEM)
     else:
         w, q, part_y = mix_x(
             thermal_field.reshape(rows, span * deep),
@@ -868,7 +939,7 @@
         ).astype(BF)
         r, factor_x, factor_z, factor_y = exchange(w, gt, mask, q, part_y, nx, ny, groups, span, per_c)
 
-    core = mix_y(r, gauss_kernel_north)
+    core, factor_x, factor_y, factor_z = mix_y(r, gauss_kernel_north, factor_x, factor_y, factor_z)
     core = core[:, :used].reshape(a_rows, per_c, -1).transpose(0, 2, 1)
     return (factor_x, factor_y, factor_z, core)
 

time: 93.3 us -> 84.3 us (0.904)
  local copies, waits for them, and re-layouts: 4.46 us -> 0 us
  Pallas kernels: 87.9 us -> 83.6 us
    unnamed x10 -> x0, local copies, waits for them, and re-layouts: 4.46 us -> none
    pallas_call x1, Pallas kernels: 7.54 us -> 4.71 us  [mix_y(): pl.pallas_call(functools.partial(mix_y_kernel, take), out_shape=(jax.Shap...]
    pallas_call x1, Pallas kernels: 80.3 us -> 78.8 us  [flow(): pl.pallas_call(functools.partial(flow_kernel, nx, ny, per_c), out_shape=(...]
where the time goes in v1:
time: 84.3 us; the launch traced here: 84.2 us
  Pallas kernels  83.6 us (99%)
    pallas_call x1, Pallas kernels, flow(): pl.pallas_call(functools.partial(flow_kernel, nx, ny, per_c), out_shape=(...  78.8 us
    pallas_call x1, Pallas kernels, mix_y(): pl.pallas_call(functools.partial(mix_y_kernel, take), out_shape=(jax.Shap...  4.71 us

profile of v1, /device:TPU:1, one launch (start us, length us, event | category | flops | bytes accessed | tf_op | source)
XLA Modules:
  0.0 84.2 jit_solution(18366288435682782462)
XLA Ops:
  0.6 78.8 %shard_map.120 = (bf16[12,384,384]{2,1,0:T(8,128)(2,1)S(1)}, f32[96,128]{1,0:T(8,128)}, f32[128,128]{1,0:T(8,128)}, f32[48,128]{1,0:T(8,128)}) custom-call(bf16[96,48,128]{2,1,0:T(8,128)(2,1)} %field.1, bf16[4,96,384]{2,1,0:T(8,128)(2,1)} %bitcast.4, bf16[384,128]{1,0:T(8,128)(2,1)} %gauss_up.1, bf16[48,384]{1,0:T(8,128)(2,1)} %constant.4.clone.select, ...), custom_call_target="tpu_custom_call" | custom-call | tf_op jit(solution)/shard_map/pallas_call | solution.py:828
  79.5 4.7 %shard_map.121 = (f32[12,384,384]{2,1,0:T(8,128)}, f32[96,128]{1,0:T(8,128)}, f32[48,128]{1,0:T(8,128)}, f32[128,128]{1,0:T(8,128)}) custom-call(bf16[12,384,384]{2,1,0:T(8,128)(2,1)S(1)} %get-tuple-element.12.r_ref, bf16[384,384]{1,0:T(8,128)(2,1)} %g_ref.1, f32[96,128]{1,0:T(8,128)} %get-tuple-element.13.fx_ref, f32[48,128]{1,0:T(8,128)} %get-tuple-element.14.fy_ref, ...), custom_call_target="tpu_custom_call" | custom-call | tf_op jit(solution)/shard_map/pallas_call | solution.py:884

commit v2 on v1

--- a/solution.py
+++ b/solution.py
@@ -449,7 +449,7 @@
     g_ref, gu_ref, sel_ref, mask_ref, east_ref, north_ref, up_ref, fx_ref, fz_ref, fy_ref,
     n_buf, t_buf, f_buf, x_buf, y_buf, w_land, wf, w_own, w_in, u_buf, wt,
     q_buf, q_in, q_all, p_buf, y_in, z_in, z_own,
-    s1, r1, l1, s2, r2, ws, wr, us, ur, ul, fs, os, ds, qs, qr, ys, yr, zs, zr, gs, gr,
+    s1, r1, l1, s2, r2, ps, pr, ws, wr, us, ur, ul, fs, os, ds, qs, qr, ys, yr, zs, zr, gs, gr,
 ):
     gx, gy = lax.axis_index("gx"), lax.axis_index("gy")
     spot, core = gy // 2, gy % 2
@@ -461,9 +461,12 @@
     spots = (end, last - spot, last - end, spot)
     goals = (gy, 2 * spot + 1 - core, 2 * end, 2 * end + 1)
 
-    span, rows, deep = f_buf.shape
-    steps, share = x_buf.shape[:2]
-    _, _, _, groups, tall, lanes = u_buf.shape
+    _, rows, deep = f_buf.shape
+    share = x_buf.shape[1]
+    span = north_ref.shape[0]
+    _, _, steps, groups, tall, lanes = u_buf.shape
+    ahead = x_buf.shape[0] - steps
+    late = steps - ahead
     a_in = mask_ref.shape[0]
     a_rows = groups * a_in
     width = up_ref.shape[1]
@@ -511,6 +514,13 @@
         to = lax.rem(gx + d, nx)
         return send(y_buf.at[m, d - 1], w_land.at[m, gx], s2.at[m, d], r2.at[m, d], (to, gy))
 
+    def early(j, way):
+        to = jnp.where(way == 0, end, last - spot)
+        return send(
+            f_buf.at[pl.ds((late + j) * tall, tall)], f_buf.at[pl.ds(span + j * tall, tall)],
+            ps.at[way, j], pr.at[j], (gx, 2 * to + core),
+        )
+
     def send_first(m):
         for d in range(1, nx + 1):
             first(m, d).start()
@@ -535,13 +545,14 @@
     def place(m, origin):
         return r_ref.at[:, pl.ds(pl.multiple_of(origin * span + m * tall, tall), tall), :]
 
-    def block(kind, slot, m):
-        source = 2 * spots[slot] + core
+    def block(kind, slot, m, chip=None):
+        chip = spots[slot] if chip is None else chip
+        source = 2 * chip + core
         if kind == 0:
             return pltpu.make_async_copy(u_buf.at[kind, slot, m], place(m, source), ul.at[slot, m])
         return send(
             u_buf.at[kind, slot, m], place(m, source), us.at[kind, slot, m],
-            ur.at[m, spots[slot], core], (gx, goals[kind]),
+            ur.at[m, chip, core], (gx, goals[kind]),
         )
 
     def arrived(m, at, side):
@@ -568,7 +579,7 @@
                     spread[:, here] * mask_ref[k : k + 1, here]
                 ).astype(BF)
 
-    def mix(kind, slot, m, left):
+    def mix(kind, slot, m, left, chip=None):
         for tile, low, high, at in pieces:
             got = jnp.dot(
                 left[:, low * deep : (high + 1) * deep],
@@ -578,7 +589,7 @@
             u_buf[kind, slot, m, :, :, tile * 128 : tile * 128 + 128] = (
                 got.reshape(groups, tall, 128).astype(BF)
             )
-        block(kind, slot, m).start()
+        block(kind, slot, m, chip).start()
 
     def settle(m):
         for d in range(1, nx):
@@ -640,8 +651,17 @@
     turn(0)
     send_first(0)
     send_first(1)
-    for c in range(1, span // batch):
+    early_sent = False
+    for c in reversed(range(1, span // batch)):
         turn(c)
+        if not early_sent and c * batch <= late * tall:
+            early_sent = True
+
+            @pl.when(middle)
+            def _():
+                for j in range(ahead):
+                    early(j, 0).start()
+                    early(j, 1).start()
     for copy in small_loads:
         copy.wait()
     sketch()
@@ -671,9 +691,11 @@
 
         @pl.when(jnp.logical_and(s < steps, middle))
         def _():
-            raw(w_own.at[s], 1, s, last - spot).start()
-            for kind in (2, 3):
-                mix(kind, 3, s, w_own.at[s])
+            @pl.when(s < late)
+            def _():
+                raw(w_own.at[s], 1, s, last - spot).start()
+                for kind in (2, 3):
+                    mix(kind, 3, s, w_own.at[s])
 
         @pl.when(jnp.logical_and(s < steps, jnp.logical_not(middle)))
         def _():
@@ -683,15 +705,45 @@
         def _():
             for kind in (1, 0):
                 mix(kind, 3, s, w_own.at[s])
+
+        @pl.when(s == 1)
+        def _():
+            for j in range(ahead):
+                early(j, 1).wait_recv()
+                send_first(steps + j)
+
+        @pl.when(jnp.logical_and(s >= 2, s < 2 + ahead))
+        def _():
+            mix_first(steps + s - 2)
+
+        @pl.when(jnp.logical_and(s >= 4, s < 4 + ahead))
+        def _():
+            settle(steps + s - 4)
+
+        @pl.when(jnp.logical_and(jnp.logical_and(s >= 4, s < 4 + ahead), jnp.logical_not(middle)))
+        def _():
+            for kind in (1, 0):
+                mix(kind, 0, late + s - 4, w_own.at[steps + s - 4], near)
 
         @pl.when(jnp.logical_and(jnp.logical_and(s >= 1, s < steps + 1), middle))
         def _():
             m = s - 1
             raw(w_own.at[m], 0, m, near).wait_recv()
             raw(w_in.at[0, m], 2, m, last - spot).start()
-            raw(w_own.at[m], 1, m, last - spot).wait_recv()
-            for kind, slot in ((2, 1), (3, 1), (1, 1), (0, 1), (1, 0), (0, 0)):
-                mix(kind, slot, m, w_in.at[slot, m])
+
+            @pl.when(m < late)
+            def _():
+                raw(w_own.at[m], 1, m, last - spot).wait_recv()
+                for kind in (2, 3, 1, 0):
+                    mix(kind, 1, m, w_in.at[1, m])
+
+            @pl.when(m >= late)
+            def _():
+                for kind in (2, 3, 1, 0):
+                    mix(kind, 1, m, w_own.at[m + ahead])
+
+            for kind in (1, 0):
+                mix(kind, 0, m, w_in.at[0, m])
 
         @pl.when(jnp.logical_and(s >= 2, middle))
         def _():
@@ -755,10 +807,14 @@
 
         @pl.when(middle)
         def _():
-            raw(w_own.at[m], 1, m, last - spot).wait_send()
             raw(w_in.at[0, m], 2, m, last - spot).wait_send()
-            block(2, 3, m).wait_send()
-            block(3, 3, m).wait_send()
+
+            @pl.when(m < late)
+            def _():
+                raw(w_own.at[m], 1, m, last - spot).wait_send()
+                block(2, 3, m).wait_send()
+                block(3, 3, m).wait_send()
+
             for slot in range(3):
                 block(0, slot, m).wait()
                 block(1, slot, m).wait_send()
@@ -772,11 +828,32 @@
             raw(w_own.at[m], 0, m, near).wait_send()
             for d in range(1, ny // 2):
                 for side in range(2):
-                    arrived(m, lax.rem(spot + d, ny // 2), side)
+                    at = lax.rem(spot + d, ny // 2)
+                    here = jnp.logical_and(jnp.logical_and(at == near, side == core), m >= late)
+
+                    @pl.when(jnp.logical_not(here))
+                    def _(at=at, side=side):
+                        arrived(m, at, side)
+
+            @pl.when(m >= late)
+            def _():
+                block(0, 0, m, near).wait()
+                block(1, 0, m, near).wait_send()
 
         return carry
 
     lax.fori_loop(0, steps, close, 0)
+    for j in range(ahead):
+        for d in range(1, nx):
+            first(steps + j, d).wait_send()
+            second(steps + j, d).wait_send()
+
+    @pl.when(middle)
+    def _():
+        for j in range(ahead):
+            early(j, 0).wait_send()
+            early(j, 1).wait_send()
+
     for copy in (done_x, done_y, done_z):
         copy.wait()
 
@@ -788,6 +865,8 @@
     groups = a_rows // a_in
     tall = 8
     steps, share = span // tall, tall // nx
+    ahead = 2
+    most = steps + ahead
     width = up.shape[1]
     x_rows, z_rows = rows // ny, deep // ny
     lane = np.arange(lanes)
@@ -808,19 +887,20 @@
         vm((rows, width), F32), vm((deep, width), F32), vm((span, width), F32),
         vm((span // batch, rows, batch, deep), BF),
         vm((rows * batch, deep), F32),
-        vm((span, rows, deep), BF),
-        vm((steps, share, nx * rows, deep), BF),
-        vm((steps, nx - 1, a_rows, share * deep), BF),
-        vm((steps, nx, a_rows, share * deep), BF),
+        vm((span + ahead * tall, rows, deep), BF),
+        vm((most, share, nx * rows, deep), BF),
+        vm((most, nx - 1, a_rows, share * deep), BF),
+        vm((most, nx, a_rows, share * deep), BF),
         vm((a_rows * tall, deep), F32),
-        vm((steps, groups * tall, a_in * deep), BF),
+        vm((most, groups * tall, a_in * deep), BF),
         vm((3, steps, groups * tall, a_in * deep), BF),
         vm((4, 4, steps, groups, tall, lanes), BF),
         vm((4, total_k, 128), BF),
         vm(q_shape, F32), vm(q_shape, F32), vm(q_shape, F32),
         vm((span, width), F32), vm((nx, span, width), F32),
         vm((nx, z_rows, width), F32), vm((z_rows, width), F32),
-        dma(steps, nx), dma(steps, nx), dma(steps), dma(steps, nx), dma(steps, nx),
+        dma(most, nx), dma(most, nx), dma(most), dma(most, nx), dma(most, nx),
+        dma(2, ahead), dma(ahead),
         dma(3, steps), dma(3, steps), dma(4, 4, steps), dma(steps, ny // 2, 2), dma(4, steps),
         dma(span // batch), dma(7), dma(3),
         dma(ny), dma(ny), dma(nx), dma(nx), dma(nx), dma(nx), dma(ny), dma(ny),
@@ -911,7 +991,7 @@
     used = a_in * per_c
     lanes = -(-used // 128) * 128
 
-    if ny == 8 and 8 % nx == 0 and span % 8 == 0 and span // 8 > 2 and a_in % 8 == 0 and per_c % 16 == 0:
+    if ny == 8 and 8 % nx == 0 and span % 8 == 0 and span // 8 > 5 and a_in % 8 == 0 and per_c % 16 == 0:
         r, factor_x, factor_z, factor_y = flow(
             thermal_field, gauss_kernel_east, gauss_kernel_upward,
             probe_range_east, probe_range_north, probe_range_upward, nx, ny, a_in, lanes,

time: 84.3 us -> 79.3 us (0.941)
  Pallas kernels: 83.6 us -> 78.5 us
    pallas_call x1, Pallas kernels: 78.8 us -> 73.8 us  [flow(): pl.pallas_call(functools.partial(flow_kernel, nx, ny, per_c), out_shape=(...]
where the time goes in v2:
time: 79.3 us; the launch traced here: 79.2 us
  Pallas kernels  78.5 us (99%)
    pallas_call x1, Pallas kernels, flow(): pl.pallas_call(functools.partial(flow_kernel, nx, ny, per_c), out_shape=(...  73.8 us
    pallas_call x1, Pallas kernels, mix_y(): pl.pallas_call(functools.partial(mix_y_kernel, take), out_shape=(jax.Shap...  4.71 us

profile of v2, /device:TPU:1, one launch (start us, length us, event | category | flops | bytes accessed | tf_op | source)
XLA Modules:
  0.0 79.2 jit_solution(12041418782000478722)
XLA Ops:
  0.6 73.8 %shard_map.120 = (bf16[12,384,384]{2,1,0:T(8,128)(2,1)S(1)}, f32[96,128]{1,0:T(8,128)}, f32[128,128]{1,0:T(8,128)}, f32[48,128]{1,0:T(8,128)}) custom-call(bf16[96,48,128]{2,1,0:T(8,128)(2,1)} %field.1, bf16[4,96,384]{2,1,0:T(8,128)(2,1)} %bitcast.4, bf16[384,128]{1,0:T(8,128)(2,1)} %gauss_up.1, bf16[48,384]{1,0:T(8,128)(2,1)} %constant.4.clone.select, ...), custom_call_target="tpu_custom_call" | custom-call | tf_op jit(solution)/shard_map/pallas_call | solution.py:908
  74.4 4.7 %shard_map.121 = (f32[12,384,384]{2,1,0:T(8,128)}, f32[96,128]{1,0:T(8,128)}, f32[48,128]{1,0:T(8,128)}, f32[128,128]{1,0:T(8,128)}) custom-call(bf16[12,384,384]{2,1,0:T(8,128)(2,1)S(1)} %get-tuple-element.12.r_ref, bf16[384,384]{1,0:T(8,128)(2,1)} %g_ref.1, f32[96,128]{1,0:T(8,128)} %get-tuple-element.13.fx_ref, f32[48,128]{1,0:T(8,128)} %get-tuple-element.14.fy_ref, ...), custom_call_target="tpu_custom_call" | custom-call | tf_op jit(solution)/shard_map/pallas_call | solution.py:964

commit v3 on v2

--- a/solution.py
+++ b/solution.py
@@ -495,6 +495,14 @@
         pl.semaphore_signal(barrier, inc=1, device_id=(gx, lax.rem(gy + d, ny)), device_id_type=MESH)
     for d in range(1, nx):
         pl.semaphore_signal(barrier, inc=1, device_id=(lax.rem(gx + d, nx), gy), device_id_type=MESH)
+
+    def turn(c):
+        loads[c].wait()
+        t_buf[...] = n_buf[c].astype(F32).reshape(rows * batch, deep)
+        for y in range(batch):
+            f_buf[c * batch + y] = t_buf[pl.ds(y, rows, stride=batch), :].astype(BF)
+
+    turn(0)
     pl.semaphore_wait(barrier, nx + ny - 2)
 
     def send(src, dst, ssem, rsem, where):
@@ -642,13 +650,6 @@
         source = lax.rem(gy - d + ny, ny)
         return send(q_all.at[source], q_all.at[source], gs.at[d], gr.at[d], (gx, source))
 
-    def turn(c):
-        loads[c].wait()
-        t_buf[...] = n_buf[c].astype(F32).reshape(rows * batch, deep)
-        for y in range(batch):
-            f_buf[c * batch + y] = t_buf[pl.ds(y, rows, stride=batch), :].astype(BF)
-
-    turn(0)
     send_first(0)
     send_first(1)
     early_sent = False

time: 79.3 us -> 79 us (level)
  no operation moved by 1% of the time
where the time goes in v3:
time: 79 us; the launch traced here: 78.9 us
  Pallas kernels  78.2 us (99%)
    pallas_call x1, Pallas kernels, flow(): pl.pallas_call(functools.partial(flow_kernel, nx, ny, per_c), out_shape=(...  73.5 us
    pallas_call x1, Pallas kernels, mix_y(): pl.pallas_call(functools.partial(mix_y_kernel, take), out_shape=(jax.Shap...  4.71 us

profile of v3, /device:TPU:1, one launch (start us, length us, event | category | flops | bytes accessed | tf_op | source)
XLA Modules:
  0.0 78.9 jit_solution(6847168180062341445)
XLA Ops:
  0.6 73.5 %shard_map.120 = (bf16[12,384,384]{2,1,0:T(8,128)(2,1)S(1)}, f32[96,128]{1,0:T(8,128)}, f32[128,128]{1,0:T(8,128)}, f32[48,128]{1,0:T(8,128)}) custom-call(bf16[96,48,128]{2,1,0:T(8,128)(2,1)} %field.1, bf16[4,96,384]{2,1,0:T(8,128)(2,1)} %bitcast.4, bf16[384,128]{1,0:T(8,128)(2,1)} %gauss_up.1, bf16[48,384]{1,0:T(8,128)(2,1)} %constant.4.clone.select, ...), custom_call_target="tpu_custom_call" | custom-call | tf_op jit(solution)/shard_map/pallas_call | solution.py:909
  74.2 4.7 %shard_map.121 = (f32[12,384,384]{2,1,0:T(8,128)}, f32[96,128]{1,0:T(8,128)}, f32[48,128]{1,0:T(8,128)}, f32[128,128]{1,0:T(8,128)}) custom-call(bf16[12,384,384]{2,1,0:T(8,128)(2,1)S(1)} %get-tuple-element.12.r_ref, bf16[384,384]{1,0:T(8,128)(2,1)} %g_ref.1, f32[96,128]{1,0:T(8,128)} %get-tuple-element.13.fx_ref, f32[48,128]{1,0:T(8,128)} %get-tuple-element.14.fy_ref, ...), custom_call_target="tpu_custom_call" | custom-call | tf_op jit(solution)/shard_map/pallas_call | solution.py:965
